TPU v7x, 512 devices: a whole 4x8x8 slice. The times are simulated.
512 devices in a mesh: dp: 32 (over x, y_hi, core), fsdp: 16 (over y_lo, z).
Axes of the slice: x: 4, y: 8 (y_hi: 4, y_lo: 2; y = y_hi * 2 + y_lo), z: 8, core: 2. Of those that a mesh axis runs over, the one named last changes fastest.
Arguments:
- hidden: bfloat16 [4, 2048, 16, 4096], P(None, 'dp', 'fsdp'), may hold values from -6 to 6
- frozen_query_rows: bfloat16 [4, 2048, 16, 2048], P(None, 'dp', 'fsdp'), may hold values from -10 to 10
- output_gradient: bfloat16 [4, 2048, 16, 2048], P(None, 'dp', 'fsdp'), may hold values from -6 to 6
- token_log_ratio: float32 [4, 2048, 16], P(None, 'dp', 'fsdp'), may hold values from -0.15625 to 0.15625
- lengths: int32 [4], replicated, may hold values from 1 to 32768, as said below
- response_win_probability: float32 [4], replicated, may hold values from 0.05 to 0.95
- cached_prompt_keys: bfloat16 [1024, 512], P('fsdp'), may hold values from -7.5 to 7.5
- cached_prompt_values: bfloat16 [1024, 512], P('fsdp'), may hold values from -6 to 6
- adapter_down_factor: bfloat16 [4096, 64], P('fsdp'), may hold values from -0.09375 to 0.09375
- adapter_up_factor: bfloat16 [64, 2048], P(None, 'fsdp'), may hold values from -0.125 to 0.125
- attention_norm_gain: bfloat16 [4096], P('fsdp'), may hold values from 0.5 to 1.5
Outputs:
- grad_down: float32 [4096, 64], P('fsdp')
- grad_up: float32 [64, 2048], P(None, 'fsdp')
- seq_ratio: float32 [4], replicated
Inputs may be any that keep to these rules, and one draw needn't show every extreme that they name: The lengths sum to 65472 and the longest is exactly 32768.
All inputs are finite; a program needn't handle non-finite values.
Results may differ from a plain program's by a relative error of at most 0.012.
Values may be sent and summed in bfloat16 or wider, within the bound.
A program may use at most 128 MiB of HBM per device.

v0:
```python
import math
import jax
import jax.numpy as jnp
from jax import lax
from jax.sharding import PartitionSpec as P

HEAD_SIZE = 128
QUERY_HEADS = 16
KEY_VALUE_HEADS = 4
target_scale = 1.0
norm_epsilon = 1e-05


def attend(query_vectors, cotangent, key_rows, value_rows):
    row_count = query_vectors.shape[0]
    queries_per_group = QUERY_HEADS // KEY_VALUE_HEADS
    score_scale = 1.0 / math.sqrt(HEAD_SIZE)
    pieces = []
    for shared_key_head in range(KEY_VALUE_HEADS):
        head_start = shared_key_head * queries_per_group * HEAD_SIZE
        head_stop = head_start + queries_per_group * HEAD_SIZE
        head_query = query_vectors[:, head_start:head_stop].reshape(
            row_count, queries_per_group, HEAD_SIZE
        )
        head_grad = cotangent[:, head_start:head_stop].reshape(
            row_count, queries_per_group, HEAD_SIZE
        )
        head_key = key_rows[:, shared_key_head * HEAD_SIZE : (shared_key_head + 1) * HEAD_SIZE]
        head_value = value_rows[:, shared_key_head * HEAD_SIZE : (shared_key_head + 1) * HEAD_SIZE]
        scores = (
            jnp.einsum("nhd,jd->nhj", head_query, head_key, preferred_element_type=jnp.float32)
            * score_scale
        )
        row_top = jnp.max(scores, axis=2, keepdims=True)
        exponent = jnp.exp(scores - row_top)
        row_total = jnp.sum(exponent, axis=2, keepdims=True)
        weights = exponent.astype(jnp.bfloat16)
        mixed_out = (
            jnp.einsum("nhj,jd->nhd", weights, head_value, preferred_element_type=jnp.float32)
            / row_total
        )
        inner_prod = jnp.sum(head_grad.astype(jnp.float32) * mixed_out, axis=2, keepdims=True)
        grad_prob = jnp.einsum(
            "nhd,jd->nhj", head_grad, head_value, preferred_element_type=jnp.float32
        )
        grad_score = (weights.astype(jnp.float32) / row_total * (grad_prob - inner_prod)).astype(
            jnp.bfloat16
        )
        query_gradient = (
            jnp.einsum("nhj,jd->nhd", grad_score, head_key, preferred_element_type=jnp.float32)
            * score_scale
        )
        pieces.append(query_gradient.reshape(row_count, queries_per_group * HEAD_SIZE))
    return jnp.concatenate(pieces, axis=1).astype(jnp.bfloat16)


def body(
    hidden,
    frozen_query_rows,
    output_gradient,
    token_log_ratio,
    lengths,
    response_win_probability,
    cached_prompt_keys,
    cached_prompt_values,
    adapter_down_factor,
    adapter_up_factor,
    attention_norm_gain,
):
    fsdp_count = lax.axis_size("fsdp")
    dp_index = lax.axis_index("dp")
    fsdp_index = lax.axis_index("fsdp")
    responses, per_device, single, feature_count = hidden.shape
    home_rows = responses * per_device
    local_rows = jnp.arange(per_device, dtype=jnp.int32)
    position = (dp_index * per_device + local_rows) * fsdp_count + fsdp_index
    is_valid = position[None, :] < lengths[:, None]
    partial_value = jnp.sum(jnp.where(is_valid, token_log_ratio[:, :, 0], 0.0), axis=1)
    seq_ratio = lax.psum(partial_value, ("dp", "fsdp"))
    weighting = 2.0 * (seq_ratio - target_scale * (response_win_probability - 0.5)) / responses
    down_full, up_full, gain_full = (
        lax.all_gather(adapter_down_factor, "fsdp", axis=0, tiled=True),
        lax.all_gather(adapter_up_factor, "fsdp", axis=1, tiled=True),
        lax.all_gather(attention_norm_gain, "fsdp", axis=0, tiled=True),
    )
    key_rows, value_rows = (
        lax.all_gather(cached_prompt_keys, "fsdp", axis=0, tiled=True),
        lax.all_gather(cached_prompt_values, "fsdp", axis=0, tiled=True),
    )
    widened = hidden.reshape(home_rows, feature_count).astype(jnp.float32)
    inverse = lax.rsqrt(jnp.mean(widened * widened, axis=1, keepdims=True) + norm_epsilon)
    normed_input = (widened * inverse * gain_full.astype(jnp.float32)).astype(jnp.bfloat16)
    lowrank_hidden = jnp.dot(normed_input, down_full, preferred_element_type=jnp.float32).astype(
        jnp.bfloat16
    )
    row_mask = is_valid.reshape(home_rows)
    row_coef = jnp.repeat(weighting, per_device)
    base_rows = frozen_query_rows.reshape(home_rows, -1)
    cotangent = jnp.where(
        row_mask[:, None],
        row_coef[:, None] * output_gradient.reshape(home_rows, -1).astype(jnp.float32),
        0.0,
    ).astype(jnp.bfloat16)
    query_vectors = (
        base_rows.astype(jnp.float32)
        + jnp.dot(lowrank_hidden, up_full, preferred_element_type=jnp.float32)
    ).astype(jnp.bfloat16)
    query_gradient = attend(query_vectors, cotangent, key_rows, value_rows)
    up_term = jnp.dot(lowrank_hidden.T, query_gradient, preferred_element_type=jnp.float32)
    gradient_lowrank = jnp.dot(
        query_gradient, up_full.T, preferred_element_type=jnp.float32
    ).astype(jnp.bfloat16)
    down_term = jnp.dot(normed_input.T, gradient_lowrank, preferred_element_type=jnp.float32)
    down_sum, up_sum = lax.psum((down_term, up_term), ("dp", "fsdp"))
    down_factor_part = adapter_down_factor.shape[0]
    up_factor_part = adapter_up_factor.shape[1]
    grad_down = lax.dynamic_slice_in_dim(
        down_sum, fsdp_index * down_factor_part, down_factor_part, 0
    )
    grad_up = lax.dynamic_slice_in_dim(up_sum, fsdp_index * up_factor_part, up_factor_part, 1)
    return (grad_down, grad_up, seq_ratio)


def solution(mesh):
    in_specs = (
        P(None, "dp", "fsdp", None),
        P(None, "dp", "fsdp", None),
        P(None, "dp", "fsdp", None),
        P(None, "dp", "fsdp"),
        P(),
        P(),
        P("fsdp", None),
        P("fsdp", None),
        P("fsdp", None),
        P(None, "fsdp"),
        P("fsdp"),
    )
    out_specs = (P("fsdp", None), P(None, "fsdp"), P())
    return jax.shard_map(body, mesh=mesh, in_specs=in_specs, out_specs=out_specs, check_vma=False)
```

profile of v0, /device:TPU:17, one launch (start us, length us, event | category | flops | bytes accessed | tf_op | source)
XLA Modules:
  0.0 574.0 jit_solution(2248930495816452318)
XLA Ops:
  9.6 105.0 %psum.21 = f32[4]{0:T(128)S(1)} all-reduce(f32[4]{0:T(128)S(1)} %get-tuple-element.5), channel_id=1, replica_groups=mesh['dp'=32,'fsdp'=16] {'dp','fsdp'}, use_global_device_ids=true, to_apply=%region_4.5 | all-reduce | flops 4 | bytes 32 | tf_op jit(solution)/shard_map/psum | solution.py:79
  116.1 2.1 multiply_reduce_fusion
  118.3 24.8 %all-gather = bf16[16,1,256]{2,1,0:T(2,128)(2,1)S(1)} all-gather(bf16[1,1,256]{2,1,0:T(2,128)(2,1)S(1)} %reshape.122), channel_id=1, replica_groups=mesh['dp'=32,'fsdp'=16] {'fsdp'}, dimensions={0}, use_global_device_ids=true | all-gather | bytes 8704 | tf_op jit(solution)/shard_map/all_gather | solution.py:84
  143.1 2.2 fusion.1
  145.7 1.3 slice_bitcast_fusion.35
  147.0 1.7 reshape.117
  148.7 1.7 reshape.114
  150.5 1.7 reshape.111
  152.9 24.4 %all_gather.17 = bf16[64,2048]{1,0:T(8,128)(2,1)S(1)} all-gather(bf16[64,128]{1,0:T(8,128)(2,1)S(1)} %copy-done.17), channel_id=1, replica_groups=mesh['dp'=32,'fsdp'=16] {'fsdp'}, dimensions={1}, use_global_device_ids=true | all-gather | bytes 278528 | tf_op jit(solution)/shard_map/all_gather | solution.py:83
  177.3 27.5 %all_gather.16 = bf16[4096,64]{0,1:T(8,128)(2,1)S(1)} all-gather(bf16[256,64]{0,1:T(8,128)(2,1)S(1)} %copy-done.16), channel_id=1, replica_groups=mesh['dp'=32,'fsdp'=16] {'fsdp'}, dimensions={0}, use_global_device_ids=true | all-gather | bytes 557056 | tf_op jit(solution)/shard_map/all_gather | solution.py:82
  207.1 1.7 multiply_reduce_fusion.4
  208.8 2.0 copy-done
  211.9 3.0 fusion.39
  216.4 1.9 multiply_reduce_fusion.1
  218.3 1.9 copy-done.1
  222.0 3.1 fusion.30
  226.6 1.8 multiply_reduce_fusion.2
  228.4 2.0 copy-done.2
  232.1 3.1 fusion.33
  236.6 1.8 multiply_reduce_fusion.3
  238.4 1.9 copy-done.3
  240.4 1.1 fusion.4
  242.3 3.1 fusion.36
  246.9 4.8 fusion.21
  251.7 4.8 fusion.24
  256.5 4.8 fusion.23
  261.3 4.8 fusion.22
  266.2 3.6 fusion.25
  269.8 2.2 fusion.70
  272.0 292.6 %all-reduce.3.cloned.1.call-done = (f32[4096,64]{0,1:T(8,128)}, f32[64,2048]{1,0:T(8,128)}) async-done(((f32[4096,64]{0,1:T(8,128)}, f32[64,2048]{1,0:T(8,128)}), (f32[4096,64]{0,1:T(8,128)}, f32[64,2048]{1,0:T(8,128)})) %all-reduce.3.cloned.1.call-update) | async-done | bytes 1572880 | tf_op jit(solution)/shard_map/psum | solution.py:114
  564.6 1.5 constant_dynamic-slice_fusion.1
  566.1 1.4 constant_dynamic-slice_fusion
  (98 shorter events, 18.6 us)
Async XLA Ops:
  7.2 138.2 %copy-start.6 = (bf16[4,64,1,2048]{3,1,2,0:T(8,128)(2,1)S(1)}, bf16[4,64,1,2048]{3,1,2,0:T(8,128)(2,1)}, u32[]{:S(2)}) copy-start(bf16[4,64,1,2048]{3,1,2,0:T(8,128)(2,1)} %param.13) | copy-start | bytes 3145732
  7.2 199.9 %all-gather.4.cloned.1.call-start = ((), (), s32[]{:S(2)}) async-start(), calls=%async_computation | async-start | bytes 1114112 | tf_op jit(solution)/shard_map/all_gather | solution.py:87
  7.9 204.0 %all-gather.6.cloned.1.call-start = ((), (), s32[]{:S(2)}) async-start(), calls=%async_computation.1 | async-start | bytes 1114112 | tf_op jit(solution)/shard_map/all_gather | solution.py:88
  8.7 555.9 %all-reduce.3.cloned.1.call-start = ((), (), s32[]{:S(2)}) async-start(), calls=%async_computation.2 | async-start | bytes 3145728 | tf_op jit(solution)/shard_map/psum | solution.py:114
  114.6 3.7 copy-start.31
  145.3 7.6 %copy-start.17 = (bf16[64,128]{1,0:T(8,128)(2,1)S(1)}, bf16[64,128]{1,0:T(8,128)(2,1)}, u32[]{:S(2)}) copy-start(bf16[64,128]{1,0:T(8,128)(2,1)} %param.20) | copy-start | bytes 49156
  145.4 32.0 %copy-start.16 = (bf16[256,64]{0,1:T(8,128)(2,1)S(1)}, bf16[256,64]{0,1:T(8,128)(2,1)}, u32[]{:S(2)}) copy-start(bf16[256,64]{0,1:T(8,128)(2,1)} %param.19) | copy-start | bytes 98308
  145.7 59.9 %copy-start.5 = (bf16[4,64,1,2048]{3,1,2,0:T(8,128)(2,1)S(1)}, bf16[4,64,1,2048]{3,1,2,0:T(8,128)(2,1)}, u32[]{:S(2)}) copy-start(bf16[4,64,1,2048]{3,1,2,0:T(8,128)(2,1)} %param.12) | copy-start | bytes 3145732
  208.8 2.0 copy-start
  210.8 4.2 copy-start.10
  211.7 6.6 %copy-start.18 = (f32[256,4]{0,1:T(4,128)}, f32[256,4]{0,1:T(4,128)S(1)}, u32[]{:S(2)}) copy-start(f32[256,4]{0,1:T(4,128)S(1)} %fusion.2) | copy-start | bytes 12292
  216.4 5.6 copy-start.4
  218.3 1.9 copy-start.1
  221.2 0.8 copy-start.19
  222.0 3.1 copy-start.9
  222.0 3.1 copy-start.11
  228.4 2.0 copy-start.2
  232.1 3.1 copy-start.8
  232.1 3.1 copy-start.12
  238.4 1.9 copy-start.3
  242.3 3.1 copy-start.7
  242.3 3.1 copy-start.13
  246.9 4.8 copy-start.20
  246.9 4.8 copy-start.25
  251.7 4.8 copy-start.22
  251.7 4.8 copy-start.26
  256.5 4.8 copy-start.24
  256.5 4.8 copy-start.27
  266.2 3.7 copy-start.15
  266.2 3.7 copy-start.28
  266.2 3.7 copy-start.29
  266.2 3.7 copy-start.30
  (3 other events, 2.2 us)
Sparse Core Ops, SparseCore 0:
  10.1 66.9 all-gather.3
  79.2 69.6 all-gather.5
  272.2 292.3 all-reduce.2
where the time goes:
time: 575 us; the launch traced here: 574 us
  waiting for transfers between devices  294 us (51%)
  blocking collectives  182 us (32%)
  matrix products  45.8 us (8%)
  local copies, waits for them, and re-layouts  25.3 us (4%)
  between operations  14.1 us (2%)
  other arithmetic  13.1 us (2%)
    psum x1, waiting for transfers between devices, body(): down_sum, up_sum = lax.psum((down_term, up_term), ('dp', 'fsdp'))  293 us
    psum x1, blocking collectives, body(): seq_ratio = lax.psum(partial_value, ('dp', 'fsdp'))  105 us
    all_gather x1, blocking collectives, body(): lax.all_gather(adapter_down_factor, 'fsdp', axis=0, tiled=True)  27.5 us
    all_gather x1, blocking collectives, body(): lax.all_gather(attention_norm_gain, 'fsdp', axis=0, tiled=True)  24.8 us
    all_gather x1, blocking collectives, body(): lax.all_gather(adapter_up_factor, 'fsdp', axis=1, tiled=True)  24.4 us
    dot_general x4, matrix products, attend(): jnp.einsum('nhj,jd->nhd', grad_score, head_key, preferred_element_type=jn...  19.2 us
    dot_general x4, matrix products, attend(): jnp.einsum('nhj,jd->nhd', weights, head_value, preferred_element_type=jnp...  12.3 us
  transfers between devices with their start and end apart: 3, of which 1 were waited for; matrix products, arithmetic and copies ran while one was open for 3% of the time, Pallas kernels for 0%

commit v1 on v0

--- a/solution.py
+++ b/solution.py
@@ -78,8 +78,16 @@
     partial_value = jnp.sum(jnp.where(is_valid, token_log_ratio[:, :, 0], 0.0), axis=1)
     seq_ratio = lax.psum(partial_value, ("dp", "fsdp"))
     weighting = 2.0 * (seq_ratio - target_scale * (response_win_probability - 0.5)) / responses
+
+    def end_the_surface(vals, axis_name):
+        r1 = jnp.concatenate(
+            lax.all_to_all(jnp.stack(lax.psum(1, axis_name) * [vals], axis=0), axis_name, 0, 0),
+            axis=0,
+        )
+        return r1
+
     down_full, up_full, gain_full = (
-        lax.all_gather(adapter_down_factor, "fsdp", axis=0, tiled=True),
+        end_the_surface(adapter_down_factor, "fsdp"),
         lax.all_gather(adapter_up_factor, "fsdp", axis=1, tiled=True),
         lax.all_gather(attention_norm_gain, "fsdp", axis=0, tiled=True),
     )

time: 575 us -> 539 us (0.937)
  waiting for transfers between devices: 294 us -> 274 us
  blocking collectives: 182 us -> 169 us
  starting transfers between devices: 0.11 us -> 11.3 us
  local copies, waits for them, and re-layouts: 25.3 us -> 14.6 us
    all_gather x1 -> x0, blocking collectives: 27.5 us -> none  [body(): lax.all_gather(adapter_down_factor, 'fsdp', axis=0, tiled=True)]
    psum x1, waiting for transfers between devices: 293 us -> 273 us  [body(): down_sum, up_sum = lax.psum((down_term, up_term), ('dp', 'fsdp'))]
    all_to_all x0 -> x1, starting transfers between devices: none -> 11.2 us  [end_the_surface(): lax.all_to_all(jnp.stack(lax.psum(1, axis_name) * [vals], axis=0), axis_n...]
    all_gather x1, blocking collectives: 24.8 us -> 34.7 us  [body(): lax.all_gather(attention_norm_gain, 'fsdp', axis=0, tiled=True)]
    unnamed x67 -> x36, local copies, waits for them, and re-layouts: 10.9 us -> 4.41 us
    reshape x4 -> x1, local copies, waits for them, and re-layouts: 5.92 us -> 0.03 us  [end_the_surface(): jnp.concatenate(lax.all_to_all(jnp.stack(lax.psum(1, axis_name) * [vals],...]
  transfers between devices with their start and end apart: 3 -> 4, of which waited for: 1 -> 1; matrix products, arithmetic and copies ran while one was open for 3% -> 5% of each run, Pallas kernels for 0% -> 0%
where the time goes in v1:
time: 539 us; the launch traced here: 538 us
  waiting for transfers between devices  274 us (51%)
  blocking collectives  169 us (31%)
  matrix products  43.4 us (8%)
  local copies, waits for them, and re-layouts  14.6 us (3%)
  between operations  14 us (3%)
  other arithmetic  11.5 us (2%)
  starting transfers between devices  11.3 us (2%)
    psum x1, waiting for transfers between devices, body(): down_sum, up_sum = lax.psum((down_term, up_term), ('dp', 'fsdp'))  273 us
    psum x1, blocking collectives, body(): seq_ratio = lax.psum(partial_value, ('dp', 'fsdp'))  108 us
    all_gather x1, blocking collectives, body(): lax.all_gather(attention_norm_gain, 'fsdp', axis=0, tiled=True)  34.7 us
    all_gather x1, blocking collectives, body(): lax.all_gather(adapter_up_factor, 'fsdp', axis=1, tiled=True)  26.3 us
    dot_general x4, matrix products, attend(): jnp.einsum('nhj,jd->nhd', grad_score, head_key, preferred_element_type=jn...  18.2 us
    dot_general x4, matrix products, attend(): jnp.einsum('nhj,jd->nhd', weights, head_value, preferred_element_type=jnp...  13 us
    all_to_all x1, starting transfers between devices, end_the_surface(): lax.all_to_all(jnp.stack(lax.psum(1, axis_name) * [vals], axis=0), axis_n...  11.2 us
  transfers between devices with their start and end apart: 4, of which 1 were waited for; matrix products, arithmetic and copies ran while one was open for 5% of the time, Pallas kernels for 0%

profile of v1, /device:TPU:17, one launch (start us, length us, event | category | flops | bytes accessed | tf_op | source)
XLA Modules:
  0.0 538.0 jit_solution(10086134916646878418)
XLA Ops:
  8.0 1.6 stack.2
  9.6 11.2 %all-to-all-start = ((bf16[16,256,64]{1,2,0:T(8,128)(2,1)}), bf16[16,256,64]{1,2,0:T(8,128)(2,1)S(1)}, u32[]{:S(2)}, u32[]{:S(2)}) async-start(bf16[16,256,64]{1,2,0:T(8,128)(2,1)} %stack.2), calls=%async_computation | async-start | bytes 1048576 | tf_op jit(solution)/shard_map/all_to_all | solution.py:84
  22.2 34.7 %all-gather = bf16[16,1,256]{2,1,0:T(2,128)(2,1)S(1)} all-gather(bf16[1,1,256]{2,1,0:T(2,128)(2,1)S(1)} %reshape.140), channel_id=1, replica_groups=mesh['dp'=32,'fsdp'=16] {'fsdp'}, dimensions={0}, use_global_device_ids=true | all-gather | bytes 8704 | tf_op jit(solution)/shard_map/all_gather | solution.py:92
  56.9 2.1 multiply_reduce_fusion
  59.1 2.0 multiply_convert_fusion.4
  61.1 26.3 %all_gather.13 = bf16[64,2048]{1,0:T(8,128)(2,1)S(1)} all-gather(bf16[64,128]{1,0:T(8,128)(2,1)S(1)} %copy-done.11), channel_id=1, replica_groups=mesh['dp'=32,'fsdp'=16] {'fsdp'}, dimensions={1}, use_global_device_ids=true | all-gather | bytes 278528 | tf_op jit(solution)/shard_map/all_gather | solution.py:91
  87.7 108.0 %psum.21 = f32[4]{0:T(128)S(1)} all-reduce(f32[4]{0:T(128)S(1)} %get-tuple-element.5), channel_id=1, replica_groups=mesh['dp'=32,'fsdp'=16] {'dp','fsdp'}, use_global_device_ids=true, to_apply=%region_4.5 | all-reduce | flops 4 | bytes 32 | tf_op jit(solution)/shard_map/psum | solution.py:79
  195.9 1.5 fusion.12
  198.3 1.8 copy.97
  200.1 1.8 copy.104
  202.9 2.0 fusion.1
  204.9 2.4 convolution_convert_fusion.1
  207.9 1.8 multiply_reduce_fusion.4
  210.6 0.9 fusion.2
  211.7 0.9 fusion.4
  213.9 0.9 fusion.6
  214.8 1.0 copy-done.3
  216.6 1.9 copy-done.1
  218.5 0.9 fusion.8
  219.5 3.2 fusion.29
  222.7 4.9 fusion.25
  227.6 3.4 fusion.30
  231.0 4.2 fusion.26
  235.2 3.2 fusion.31
  238.4 4.1 fusion.27
  242.6 3.2 fusion.32
  245.8 5.0 fusion.28
  250.8 2.2 fusion.54
  253.0 2.9 fusion.33
  255.9 272.6 %all-reduce.3.cloned.1.call-done = (f32[4096,64]{0,1:T(8,128)}, f32[64,2048]{1,0:T(8,128)}) async-done(((f32[4096,64]{0,1:T(8,128)}, f32[64,2048]{1,0:T(8,128)}), (f32[4096,64]{0,1:T(8,128)}, f32[64,2048]{1,0:T(8,128)})) %all-reduce.3.cloned.1.call-update) | async-done | bytes 1572880 | tf_op jit(solution)/shard_map/psum | solution.py:122
  528.6 1.5 constant_dynamic-slice_fusion.1
  530.1 1.4 constant_dynamic-slice_fusion
  (60 shorter events, 8.2 us)
Async XLA Ops:
  7.2 52.0 %copy-start = (bf16[4,64,1,4096]{3,1,2,0:T(8,128)(2,1)S(1)}, bf16[4,64,1,4096]{3,1,2,0:T(8,128)(2,1)}, u32[]{:S(2)}) copy-start(bf16[4,64,1,4096]{3,1,2,0:T(8,128)(2,1)} %param.11) | copy-start | bytes 6291460
  7.2 54.0 %copy-start.11 = (bf16[64,128]{1,0:T(8,128)(2,1)S(1)}, bf16[64,128]{1,0:T(8,128)(2,1)}, u32[]{:S(2)}) copy-start(bf16[64,128]{1,0:T(8,128)(2,1)} %param.20) | copy-start | bytes 49156
  7.2 80.3 %copy-start.12 = (f32[4,64,1]{1,2,0:T(1,128)S(1)}, f32[4,64,1]{1,2,0:T(1,128)}, u32[]{:S(2)}) copy-start(f32[4,64,1]{1,2,0:T(1,128)} %param.14) | copy-start | bytes 3076
  7.2 80.3 %copy-start.13 = (s32[4]{0:T(128)S(1)}, s32[4]{0:T(128)}, u32[]{:S(2)}) copy-start(s32[4]{0:T(128)} %param.15) | copy-start | bytes 52
  7.2 188.5 %copy-start.14 = (f32[4]{0:T(128)S(1)}, f32[4]{0:T(128)}, u32[]{:S(2)}) copy-start(f32[4]{0:T(128)} %param.16) | copy-start | bytes 52
  7.2 200.7 %all-gather.4.cloned.1.call-start = ((), (), s32[]{:S(2)}) async-start(), calls=%async_computation.1 | async-start | bytes 1114112 | tf_op jit(solution)/shard_map/all_gather | solution.py:95
  9.6 195.3 %all-to-all-start = ((bf16[16,256,64]{1,2,0:T(8,128)(2,1)}), bf16[16,256,64]{1,2,0:T(8,128)(2,1)S(1)}, u32[]{:S(2)}, u32[]{:S(2)}) async-start(bf16[16,256,64]{1,2,0:T(8,128)(2,1)} %stack.2), calls=%async_computation | async-start | bytes 1048576 | tf_op jit(solution)/shard_map/all_to_all | solution.py:84
  20.7 198.8 %all-gather.6.cloned.1.call-start = ((), (), s32[]{:S(2)}) async-start(), calls=%async_computation.2 | async-start | bytes 1114112 | tf_op jit(solution)/shard_map/all_gather | solution.py:96
  21.5 507.1 %all-reduce.3.cloned.1.call-start = ((), (), s32[]{:S(2)}) async-start(), calls=%async_computation.3 | async-start | bytes 3145728 | tf_op jit(solution)/shard_map/psum | solution.py:122
  195.7 9.2 %copy-start.16 = (f32[4]{0:T(128)}, f32[4]{0:T(128)S(1)}, u32[]{:S(2)}) copy-start(f32[4]{0:T(128)S(1)} %psum.21) | copy-start | bytes 52
  204.9 2.5 copy-start.6
  207.9 1.8 copy-start.7
  209.8 2.0 copy-start.4
  210.6 2.5 copy-start.2
  213.8 2.0 copy-start.3
  215.8 3.7 copy-start.10
  216.6 1.9 copy-start.1
  222.7 4.9 copy-start.9
  231.0 4.2 copy-start.8
  245.8 5.0 copy-start.15
  245.8 7.2 %copy-start.5 = (bf16[256,4096]{1,0:T(8,128)(2,1)S(1)}, bf16[256,4096]{1,0:T(8,128)(2,1)}, u32[]{:S(2)}) copy-start(bf16[256,4096]{1,0:T(8,128)(2,1)} %fusion.1) | copy-start | bytes 6291460
Sparse Core Ops, SparseCore 0:
  10.1 67.7 all-gather.3
  80.0 69.3 all-gather.5
  256.1 272.4 all-reduce.2
